TPU v7x, 32 devices: a whole 2x2x4 slice. The times are simulated.
32 devices in a mesh: row: 8 (over z, x), col: 4 (over y, core).
Axes of the slice: x: 2, y: 2, z: 4, core: 2. Of those that a mesh axis runs over, the one named last changes fastest.
Arguments:
- krylov_block: bfloat16 [64, 16384], P(None, ('row', 'col')), may hold values from -54 to 54
- degree: int32 [16384], P(('row', 'col')), may hold values from 16 to 64
- tile_values: bfloat16 [256, 4, 64, 512], P('row', 'col'), may hold values from -6 to 6
- tile_column: int32 [256, 4, 8], P('row', 'col'), may hold values from 0 to 63
- tile_live: int32 [256, 4, 8], P('row', 'col'), may hold values 0 or 1
Outputs:
- orthonormal: float32 [64, 16384], P(None, ('row', 'col'))
- quotient: float32 [64, 64], replicated
All inputs are finite; a program needn't handle non-finite values. No bound on the sum of `tile_live` on one device may be relied on, other than what follows from the above.
Results may differ from a plain program's by a relative error of at most 0.0032.
Values may be sent and summed in bfloat16 or wider, within the bound.
No kernel may reach another device: no remote copies, remote signals or barrier semaphores. Data moves between devices by JAX's collectives and lax.ppermute only.
A program may use at most 128 MiB of HBM per device.

v0:
```python
import math
import jax
import jax.numpy as jnp
from jax import lax
from jax.sharding import PartitionSpec as P


def gram_of(left, right):
    return lax.dot_general(
        left,
        right,
        (((1,), (1,)), ((), ())),
        precision=lax.Precision.HIGHEST,
        preferred_element_type=jnp.float32,
    )


def on_device(krylov_block, degree, tile_values, tile_column, tile_live):
    vectors = krylov_block.shape[0]
    owned_rows = krylov_block.shape[1]
    block_rows = tile_values.shape[0]
    height = tile_values.shape[2]
    slot_width = tile_values.shape[3]
    sources = lax.axis_size("row")
    groups = lax.axis_size("col")
    per_piece = owned_rows // height
    inv_root = lax.rsqrt(degree.astype(jnp.float32))
    basis_wide = krylov_block.astype(jnp.float32)
    scaled = (basis_wide * inv_root[None, :]).astype(jnp.bfloat16)
    gathered = lax.all_gather(scaled, "row", axis=1, tiled=True)
    blocks = gathered.reshape(vectors, sources * per_piece, height)
    pick_index = tile_column[:, 0, :].reshape(-1)
    chosen = jnp.take(blocks, pick_index, axis=1)
    chosen = chosen * tile_live[:, 0, :].reshape(1, -1, 1).astype(jnp.bfloat16)
    chosen = chosen.reshape(vectors, block_rows, slot_width)
    panel = tile_values[:, 0]
    whole_rows = jnp.einsum("klc,luc->klu", chosen, panel, preferred_element_type=jnp.float32)
    whole_rows = whole_rows.reshape(vectors, block_rows * height)
    spread = lax.psum_scatter(whole_rows, "col", scatter_dimension=1, tiled=True)
    applied = basis_wide - inv_root[None, :] * spread
    quotient, energy = lax.psum(
        (gram_of(basis_wide, applied), gram_of(applied, applied)), ("row", "col")
    )
    factor = jnp.linalg.cholesky(energy)
    identity = jnp.eye(vectors, dtype=jnp.float32)
    inverse = lax.linalg.triangular_solve(factor, identity, left_side=True, lower=True)
    total_rows = sources * groups * owned_rows
    orthonormal = jnp.dot(inverse, applied, precision=lax.Precision.HIGHEST) * math.sqrt(total_rows)
    return (orthonormal, quotient / total_rows)


def solution(mesh):
    return jax.shard_map(
        on_device,
        mesh=mesh,
        in_specs=(
            P(None, ("row", "col")),
            P(("row", "col")),
            P("row", "col", None, None),
            P("row", "col", None),
            P("row", "col", None),
        ),
        out_specs=(P(None, ("row", "col")), P()),
        check_vma=False,
    )
```

profile of v0, /device:TPU:0, one launch (start us, length us, event | category | flops | bytes accessed | tf_op | source)
XLA Modules:
  0.0 156.6 jit_solution(8631686106743871151)
XLA Ops:
  7.2 0.0 copy-start
  7.2 0.0 reduce-scatter.2.cloned.1.call-start
  7.2 0.9 copy.22
  8.1 0.7 compare_and_fusion
  8.8 0.7 convert_rsqrt_fusion
  9.5 0.9 fusion.8
  10.4 33.0 %all_gather.3 = bf16[64,4096]{1,0:T(8,128)(2,1)S(1)} all-gather(bf16[64,512]{1,0:T(8,128)(2,1)S(1)} %fusion.8), channel_id=1, replica_groups=mesh['row'=8,'col'=4] {'row'}, dimensions={1}, use_global_device_ids=true | all-gather | bytes 589824 | tf_op jit(solution)/shard_map/all_gather | solution.py:30
  43.4 2.1 %reshape.72 = bf16[64,64,64]{2,1,0:T(8,128)(2,1)} reshape(bf16[64,4096]{1,0:T(8,128)(2,1)S(1)} %all_gather.3) | data formatting | bytes 1048576 | tf_op jit(solution)/shard_map/reshape | solution.py:31
  45.5 1.9 %copy.23 = bf16[64,64,64]{2,0,1:T(8,128)(2,1)S(1)} copy(bf16[64,64,64]{2,1,0:T(8,128)(2,1)} %reshape.72) | data formatting | bytes 1048576 | tf_op jit(solution)/shard_map/reshape | solution.py:31
  47.4 0.1 reshape_squeeze.7
  47.5 3.1 %gather_fusion = bf16[256,64,64]{2,1,0:T(8,128)(2,1)} fusion(bf16[64,64,64]{2,0,1:T(8,128)(2,1)S(1)} %copy.23, s32[1024]{0:T(1024)S(1)} %pad_clamp_fusion), kind=kCustom, calls=%fused_computation | custom fusion | bytes 4195328 | tf_op jit(solution)/shard_map/jit(_take)/gather | solution.py:33
  50.6 6.8 %copy.24 = bf16[64,256,64]{2,1,0:T(8,128)(2,1)} copy(bf16[64,256,64]{2,0,1:T(8,128)(2,1)} %bitcast.30) | data formatting | bytes 4194304 | tf_op jit(solution)/shard_map/jit(_take)/gather | solution.py:33
  57.4 0.0 copy-start.2
  57.4 6.5 %gather.7 = bf16[64,32,512]{2,1,0:T(8,128)(2,1)} reshape(bf16[64,256,64]{2,1,0:T(8,128)(2,1)} %copy.24) | data formatting | bytes 4194304 | tf_op jit(solution)/shard_map/jit(_take)/gather | solution.py:33
  63.9 0.0 copy-done.2
  63.9 0.1 copy.25
  64.0 0.1 mul.35
  64.1 0.1 mul.36
  64.2 0.1 copy.21
  64.3 0.1 broadcast_in_dim.18
  64.4 0.1 broadcast_in_dim.19
  64.5 1.8 %select_multiply_fusion = bf16[64,32,512]{2,1,0:T(8,128)(2,1)S(1)} fusion(bf16[64,32,512]{2,1,0:T(8,128)(2,1)} %gather.7, pred[32,512]{1,0:T(8,128)(4,1)S(1)} %broadcast_in_dim.19, bf16[32,512]{1,0:T(8,128)(2,1)S(1)} %mul.36), kind=kLoop, calls=%fused_computation.4 | loop fusion | flops 2097152 | bytes 4243456 | tf_op jit(solution)/shard_map/mul | solution.py:34
  66.3 0.0 copy-done
  66.3 1.4 fusion.3
  67.7 0.0 copy-start.1
  67.7 0.6 copy.27
  68.4 1.1 reshape.73
  69.5 0.0 reduce-scatter.2.cloned.1.call-update
  69.5 22.9 %reduce-scatter.2.cloned.1.call-done = f32[64,512]{1,0:T(8,128)} async-done(((f32[64,2048]{1,0:T(8,128)}), f32[64,512]{1,0:T(8,128)}) %reduce-scatter.2.cloned.1.call-update) | async-done | bytes 131088 | tf_op jit(solution)/shard_map/reduce_scatter | solution.py:39
  92.5 0.0 copy-done.1
  92.5 1.1 convolution_bitcast_fusion
  93.6 1.3 fusion.9
  94.8 40.0 %all-reduce = (f32[64,64]{0,1:T(8,128)S(1)}, f32[64,64]{0,1:T(8,128)S(1)}) all-reduce(f32[64,64]{0,1:T(8,128)S(1)} %fusion.9, f32[64,64]{0,1:T(8,128)S(1)} %convolution_bitcast_fusion), channel_id=1, replica_groups=mesh['row'=8,'col'=4] {'row','col'}, use_global_device_ids=true, to_apply=%region_1.2 | all-reduce | flops 8192 | bytes 65536 | tf_op jit(solution)/shard_map/psum | solution.py:41
  134.8 0.1 copy.29
  134.9 5.8 %cholesky.17 = f32[64,64]{1,0:T(8,128)S(1)} custom-call(f32[64,64]{1,0:T(8,128)S(1)} %fusion.16), custom_call_target="Cholesky" | custom-call | tf_op jit(solution)/shard_map/jit(cholesky)/cholesky | solution.py:44
  140.8 0.6 compare_reduce_fusion
  141.4 0.7 fusion.13
  142.1 4.9 %custom-call.6 = f32[1,64,64]{1,2,0:T(8,128)S(1)} custom-call(f32[1,64,64]{2,1,0:T(8,128)S(1)} %fusion.13), custom_call_target="InvertDiagBlocksLowerTriangular" | custom-call | tf_op jit(solution)/shard_map/triangular_solve | solution.py:46
  147.0 0.2 fusion.14
  147.3 0.7 copy.30
  148.0 1.8 %convolution_multiply_fusion = f32[64,512]{1,0:T(8,128)} fusion(f32[64,64]{1,0:T(8,128)S(1)} %fusion.14, bf16[64,512]{1,0:T(8,128)(2,1)S(1)} %copy-done.1, f32[64,512]{1,0:T(8,128)} %reduce-scatter.2.cloned.1.call-done, f32[512]{0:T(512)S(1)} %convert_rsqrt_fusion), kind=kOutput, calls=%fused_computation.6 | convolution fusion | flops 25296896 | bytes 346112 | tf_op jit(solution)/shard_map/dot_general | solution.py:48
  (6 shorter events, 0.1 us)
Async XLA Ops:
  7.2 59.1 %copy-start = (bf16[32,1,64,512]{3,2,1,0:T(8,128)(2,1)S(1)}, bf16[32,1,64,512]{3,2,1,0:T(8,128)(2,1)}, u32[]{:S(2)}) copy-start(bf16[32,1,64,512]{3,2,1,0:T(8,128)(2,1)} %param.7) | copy-start | bytes 6291460
  7.2 85.3 %reduce-scatter.2.cloned.1.call-start = ((), (), s32[]{:S(2)}) async-start(), calls=%async_computation.1 | async-start | bytes 655360 | tf_op jit(solution)/shard_map/reduce_scatter | solution.py:39
  57.4 6.5 %copy-start.2 = (s32[32,1,8]{0,2,1:T(8,128)S(1)}, s32[32,1,8]{0,2,1:T(8,128)}, u32[]{:S(2)}) copy-start(s32[32,1,8]{0,2,1:T(8,128)} %param.9) | copy-start | bytes 3076
  67.7 24.7 %copy-start.1 = (bf16[64,512]{1,0:T(8,128)(2,1)S(1)}, bf16[64,512]{1,0:T(8,128)(2,1)}, u32[]{:S(2)}) copy-start(bf16[64,512]{1,0:T(8,128)(2,1)} %param.5) | copy-start | bytes 196612
Sparse Core Ops, SparseCore 0:
  69.7 22.7 reduce-scatter.1
where the time goes:
time: 157 us
  blocking collectives  73 us (46%)
  local copies, waits for them, and re-layouts  24.5 us (16%)
  waiting for transfers between devices  22.9 us (15%)
  other arithmetic  16.1 us (10%)
  between operations  14.1 us (9%)
  matrix products  5.85 us (4%)
    psum x1, blocking collectives, on_device(): lax.psum((gram_of(basis_wide, applied), gram_of(applied, applied)), ('row...  40 us
    all_gather x1, blocking collectives, on_device(): gathered = lax.all_gather(scaled, 'row', axis=1, tiled=True)  33 us
    reduce_scatter x1, waiting for transfers between devices, on_device(): lax.psum_scatter(whole_rows, 'col', scatter_dimension=1, tiled=True)  22.9 us
    gather x3, local copies, waits for them, and re-layouts, on_device(): chosen = jnp.take(blocks, pick_index, axis=1)  16.3 us
    another operation x3, other arithmetic, on_device(): factor = jnp.linalg.cholesky(energy)  6.52 us
    another operation x2, other arithmetic, on_device(): lax.linalg.triangular_solve(factor, identity, left_side=True, lower=True)  5.55 us
    reshape x2, local copies, waits for them, and re-layouts, on_device(): blocks = gathered.reshape(vectors, sources * per_piece, height)  4.01 us
  transfers between devices with their start and end apart: 1, of which 1 were waited for; matrix products, arithmetic and copies ran while one was open for 0% of the time, Pallas kernels for 0%

commit v1 on v0

--- a/solution.py
+++ b/solution.py
@@ -3,6 +3,29 @@
 import jax.numpy as jnp
 from jax import lax
 from jax.sharding import PartitionSpec as P
+
+
+def cut_the_squares(chunk, array_axis):
+    high = list(chunk.shape[1:])
+    high[array_axis] *= chunk.shape[0]
+    top = jnp.moveaxis(chunk, 0, array_axis).reshape(high)
+    return top
+
+
+def measure_the_object(block_in, axis_name):
+    step_out = lax.psum(1, axis_name=axis_name)
+    earlier = lax.axis_index(axis_name)
+    far_arr, u_next = (step_out, earlier)
+    work_now, aux = (block_in[None], 1)
+    while aux < far_arr:
+        mat_out = lax.ppermute(
+            work_now, axis_name=axis_name, perm=[(pp, pp ^ aux) for pp in range(far_arr)]
+        )
+        taken_in = u_next & aux == 0
+        last = jnp.where(taken_in, work_now, mat_out)
+        work_now = jnp.concatenate([last, jnp.where(taken_in, mat_out, work_now)])
+        aux *= 2
+    return work_now
 
 
 def gram_of(left, right):
@@ -27,7 +50,8 @@
     inv_root = lax.rsqrt(degree.astype(jnp.float32))
     basis_wide = krylov_block.astype(jnp.float32)
     scaled = (basis_wide * inv_root[None, :]).astype(jnp.bfloat16)
-    gathered = lax.all_gather(scaled, "row", axis=1, tiled=True)
+    small = measure_the_object(scaled, "row")
+    gathered = cut_the_squares(small, 1)
     blocks = gathered.reshape(vectors, sources * per_piece, height)
     pick_index = tile_column[:, 0, :].reshape(-1)
     chosen = jnp.take(blocks, pick_index, axis=1)

time: 157 us -> 146 us (0.930)
  blocking collectives: 73 us -> 40 us
  waiting for transfers between devices: 22.9 us -> 34.9 us
  starting transfers between devices: 0.04 us -> 8.31 us
  other arithmetic: 16.1 us -> 18 us
    all_gather x1 -> x0, blocking collectives: 33 us -> none  [on_device(): gathered = lax.all_gather(scaled, 'row', axis=1, tiled=True)]
    ppermute x0 -> x3, waiting for transfers between devices: none -> 12 us  [measure_the_object(): lax.ppermute(work_now, axis_name=axis_name, perm=[(pp, pp ^ aux) for pp i...]
    ppermute x0 -> x3, starting transfers between devices: none -> 8.27 us  [measure_the_object(): lax.ppermute(work_now, axis_name=axis_name, perm=[(pp, pp ^ aux) for pp i...]
    reshape x2 -> x0, local copies, waits for them, and re-layouts: 4.01 us -> none  [on_device(): blocks = gathered.reshape(vectors, sources * per_piece, height)]
    another operation x0 -> x2, local copies, waits for them, and re-layouts: none -> 3.44 us  [on_device(): blocks = gathered.reshape(vectors, sources * per_piece, height)]
  transfers between devices with their start and end apart: 1 -> 4, of which waited for: 1 -> 4; matrix products, arithmetic and copies ran while one was open for 0% -> 2% of each run, Pallas kernels for 0% -> 0%
where the time goes in v1:
time: 146 us; the launch traced here: 145 us
  blocking collectives  40 us (27%)
  waiting for transfers between devices  34.9 us (24%)
  local copies, waits for them, and re-layouts  24.1 us (17%)
  other arithmetic  18 us (12%)
  between operations  14.2 us (10%)
  starting transfers between devices  8.31 us (6%)
  matrix products  5.85 us (4%)
    psum x1, blocking collectives, on_device(): lax.psum((gram_of(basis_wide, applied), gram_of(applied, applied)), ('row...  40 us
    reduce_scatter x1, waiting for transfers between devices, on_device(): lax.psum_scatter(whole_rows, 'col', scatter_dimension=1, tiled=True)  23 us
    gather x3, local copies, waits for them, and re-layouts, on_device(): chosen = jnp.take(blocks, pick_index, axis=1)  16.3 us
    ppermute x3, waiting for transfers between devices, measure_the_object(): lax.ppermute(work_now, axis_name=axis_name, perm=[(pp, pp ^ aux) for pp i...  12 us
    ppermute x3, starting transfers between devices, measure_the_object(): lax.ppermute(work_now, axis_name=axis_name, perm=[(pp, pp ^ aux) for pp i...  8.27 us
    another operation x3, other arithmetic, on_device(): factor = jnp.linalg.cholesky(energy)  6.52 us
    another operation x2, other arithmetic, on_device(): lax.linalg.triangular_solve(factor, identity, left_side=True, lower=True)  5.55 us
    another operation x2, local copies, waits for them, and re-layouts, on_device(): blocks = gathered.reshape(vectors, sources * per_piece, height)  3.44 us
  transfers between devices with their start and end apart: 4, of which 4 were waited for; matrix products, arithmetic and copies ran while one was open for 2% of the time, Pallas kernels for 0%

profile of v1, /device:TPU:0, one launch (start us, length us, event | category | flops | bytes accessed | tf_op | source)
XLA Modules:
  0.0 145.4 jit_solution(439240201845718929)
XLA Ops:
  7.2 0.0 copy-start
  7.2 0.0 reduce-scatter.2.cloned.1.call-start
  7.2 0.8 convert_rsqrt_fusion
  8.1 0.9 fusion.10
  8.9 3.0 %collective-permute-start = (bf16[1,64,512]{2,1,0:T(8,128)(2,1)S(1)}, bf16[1,64,512]{2,1,0:T(8,128)(2,1)S(1)}, u32[]{:S(2)}, u32[]{:S(2)}) collective-permute-start(bf16[1,64,512]{2,1,0:T(8,128)(2,1)S(1)} %fusion.10), channel_id=1, source_target_pairs={{0,4},{4,0},{8,12},{12,8},{16,20},{20,16},{24,28},{28,24},{1,5},{5... | collective-permute-start | bytes 196616 | tf_op jit(solution)/shard_map/ppermute | solution.py:21
  11.9 0.7 convert_bitcast_fusion
  12.6 0.8 copy.14
  13.4 0.1 reshape_squeeze.7
  13.5 0.1 copy.17
  13.5 0.1 mul.35
  13.7 0.1 mul.36
  13.8 0.4 collective-permute-done
  14.2 0.9 broadcast_select_fusion.5
  15.1 2.2 %collective-permute-start.1 = (bf16[2,64,512]{2,1,0:T(8,128)(2,1)S(1)}, bf16[2,64,512]{2,1,0:T(8,128)(2,1)S(1)}, u32[]{:S(2)}, u32[]{:S(2)}) collective-permute-start(bf16[2,64,512]{2,1,0:T(8,128)(2,1)S(1)} %pad_maximum_fusion.1), channel_id=1, source_target_pairs={{0,8},{4,12},{8,0},{12,4},{16,24},{20,28},{24,16},{28,20},{1,9},{5... | collective-permute-start | bytes 393224 | tf_op jit(solution)/shard_map/ppermute | solution.py:21
  17.2 0.7 compare_and_fusion
  17.9 0.1 copy.12
  18.0 0.1 broadcast_in_dim.21
  18.1 0.1 broadcast_in_dim.22
  18.2 1.9 %collective-permute-done.1 = bf16[2,64,512]{2,1,0:T(8,128)(2,1)S(1)} collective-permute-done((bf16[2,64,512]{2,1,0:T(8,128)(2,1)S(1)}, bf16[2,64,512]{2,1,0:T(8,128)(2,1)S(1)}, u32[]{:S(2)}, u32[]{:S(2)}) %collective-permute-start.1) | collective-permute-done | bytes 131104 | tf_op jit(solution)/shard_map/ppermute | solution.py:21
  20.2 3.1 %collective-permute-start.2 = (bf16[4,64,512]{2,1,0:T(8,128)(2,1)S(1)}, bf16[4,64,512]{2,1,0:T(8,128)(2,1)S(1)}, u32[]{:S(2)}, u32[]{:S(2)}) collective-permute-start(bf16[4,64,512]{2,1,0:T(8,128)(2,1)S(1)} %pad_maximum_fusion), channel_id=1, source_target_pairs={{0,16},{4,20},{8,24},{12,28},{16,0},{20,4},{24,8},{28,12},{1,17},{... | collective-permute-start | bytes 786440 | tf_op jit(solution)/shard_map/ppermute | solution.py:21
  23.3 9.6 %collective-permute-done.2 = bf16[4,64,512]{2,1,0:T(8,128)(2,1)S(1)} collective-permute-done((bf16[4,64,512]{2,1,0:T(8,128)(2,1)S(1)}, bf16[4,64,512]{2,1,0:T(8,128)(2,1)S(1)}, u32[]{:S(2)}, u32[]{:S(2)}) %collective-permute-start.2) | collective-permute-done | bytes 262176 | tf_op jit(solution)/shard_map/ppermute | solution.py:21
  33.1 0.3 copy.13
  33.4 1.5 %reshape_reshape.3 = bf16[64,64,64]{2,1,0:T(8,128)(2,1)} reshape(bf16[64,8,512]{2,1,0:T(8,128)(2,1)S(1)} %copy.13) | data formatting | bytes 1048576 | tf_op jit(solution)/shard_map/reshape;reshape | solution.py:55
  34.9 1.9 %copy.15 = bf16[64,64,64]{2,0,1:T(8,128)(2,1)S(1)} copy(bf16[64,64,64]{2,1,0:T(8,128)(2,1)} %reshape_reshape.3) | data formatting | bytes 1048576 | tf_op jit(solution)/shard_map/reshape;reshape | solution.py:55
  36.8 3.1 %gather_fusion = bf16[256,64,64]{2,1,0:T(8,128)(2,1)} fusion(bf16[64,64,64]{2,0,1:T(8,128)(2,1)S(1)} %copy.15, s32[1024]{0:T(1024)S(1)} %pad_clamp_fusion), kind=kCustom, calls=%fused_computation | custom fusion | bytes 4195328 | tf_op jit(solution)/shard_map/jit(_take)/gather | solution.py:57
  39.9 6.8 %copy.16 = bf16[64,256,64]{2,1,0:T(8,128)(2,1)} copy(bf16[64,256,64]{2,0,1:T(8,128)(2,1)} %bitcast.36) | data formatting | bytes 4194304 | tf_op jit(solution)/shard_map/jit(_take)/gather | solution.py:57
  46.7 6.5 %gather.7 = bf16[64,32,512]{2,1,0:T(8,128)(2,1)} reshape(bf16[64,256,64]{2,1,0:T(8,128)(2,1)} %copy.16) | data formatting | bytes 4194304 | tf_op jit(solution)/shard_map/jit(_take)/gather | solution.py:57
  53.2 1.8 %select_multiply_fusion = bf16[64,32,512]{2,1,0:T(8,128)(2,1)S(1)} fusion(bf16[64,32,512]{2,1,0:T(8,128)(2,1)} %gather.7, pred[32,512]{1,0:T(8,128)(4,1)S(1)} %broadcast_in_dim.22, bf16[32,512]{1,0:T(8,128)(2,1)S(1)} %mul.36), kind=kLoop, calls=%fused_computation.4 | loop fusion | flops 2097152 | bytes 4243456 | tf_op jit(solution)/shard_map/mul | solution.py:58
  54.9 0.0 copy-done
  55.0 1.4 fusion.3
  56.4 0.0 copy-start.1
  56.4 0.6 copy.19
  57.0 1.1 reshape.69
  58.2 0.0 reduce-scatter.2.cloned.1.call-update
  58.2 23.0 %reduce-scatter.2.cloned.1.call-done = f32[64,512]{1,0:T(8,128)} async-done(((f32[64,2048]{1,0:T(8,128)}), f32[64,512]{1,0:T(8,128)}) %reduce-scatter.2.cloned.1.call-update) | async-done | bytes 131088 | tf_op jit(solution)/shard_map/reduce_scatter | solution.py:63
  81.2 0.0 copy-done.1
  81.2 1.1 convolution_bitcast_fusion
  82.3 1.3 fusion.9
  83.5 40.0 %all-reduce = (f32[64,64]{0,1:T(8,128)S(1)}, f32[64,64]{0,1:T(8,128)S(1)}) all-reduce(f32[64,64]{0,1:T(8,128)S(1)} %fusion.9, f32[64,64]{0,1:T(8,128)S(1)} %convolution_bitcast_fusion), channel_id=1, replica_groups=mesh['row'=8,'col'=4] {'row','col'}, use_global_device_ids=true, to_apply=%region_1.2 | all-reduce | flops 8192 | bytes 65536 | tf_op jit(solution)/shard_map/psum | solution.py:65
  123.5 0.1 copy.21
  123.6 5.8 %cholesky.17 = f32[64,64]{1,0:T(8,128)S(1)} custom-call(f32[64,64]{1,0:T(8,128)S(1)} %fusion.17), custom_call_target="Cholesky" | custom-call | tf_op jit(solution)/shard_map/jit(cholesky)/cholesky | solution.py:68
  129.5 0.6 compare_reduce_fusion
  130.2 0.7 fusion.14
  130.8 4.9 %custom-call.6 = f32[1,64,64]{1,2,0:T(8,128)S(1)} custom-call(f32[1,64,64]{2,1,0:T(8,128)S(1)} %fusion.14), custom_call_target="InvertDiagBlocksLowerTriangular" | custom-call | tf_op jit(solution)/shard_map/triangular_solve | solution.py:70
  135.7 0.2 fusion.15
  136.0 0.7 copy.22
  136.7 1.8 %convolution_multiply_fusion = f32[64,512]{1,0:T(8,128)} fusion(f32[64,64]{1,0:T(8,128)S(1)} %fusion.15, bf16[64,512]{1,0:T(8,128)(2,1)S(1)} %copy-done.1, f32[64,512]{1,0:T(8,128)} %reduce-scatter.2.cloned.1.call-done, f32[512]{0:T(512)S(1)} %convert_rsqrt_fusion), kind=kOutput, calls=%fused_computation.6 | convolution fusion | flops 25296896 | bytes 346112 | tf_op jit(solution)/shard_map/dot_general | solution.py:72
  (10 shorter events, 0.2 us)
Async XLA Ops:
  7.2 47.8 %copy-start = (bf16[32,1,64,512]{3,2,1,0:T(8,128)(2,1)S(1)}, bf16[32,1,64,512]{3,2,1,0:T(8,128)(2,1)}, u32[]{:S(2)}) copy-start(bf16[32,1,64,512]{3,2,1,0:T(8,128)(2,1)} %param.7) | copy-start | bytes 6291460
  7.2 74.0 %reduce-scatter.2.cloned.1.call-start = ((), (), s32[]{:S(2)}) async-start(), calls=%async_computation.1 | async-start | bytes 655360 | tf_op jit(solution)/shard_map/reduce_scatter | solution.py:63
  8.9 5.2 %collective-permute-start = (bf16[1,64,512]{2,1,0:T(8,128)(2,1)S(1)}, bf16[1,64,512]{2,1,0:T(8,128)(2,1)S(1)}, u32[]{:S(2)}, u32[]{:S(2)}) collective-permute-start(bf16[1,64,512]{2,1,0:T(8,128)(2,1)S(1)} %fusion.10), channel_id=1, source_target_pairs={{0,4},{4,0},{8,12},{12,8},{16,20},{20,16},{24,28},{28,24},{1,5},{5... | collective-permute-start | bytes 196616 | tf_op jit(solution)/shard_map/ppermute | solution.py:21
  15.1 5.1 %collective-permute-start.1 = (bf16[2,64,512]{2,1,0:T(8,128)(2,1)S(1)}, bf16[2,64,512]{2,1,0:T(8,128)(2,1)S(1)}, u32[]{:S(2)}, u32[]{:S(2)}) collective-permute-start(bf16[2,64,512]{2,1,0:T(8,128)(2,1)S(1)} %pad_maximum_fusion.1), channel_id=1, source_target_pairs={{0,8},{4,12},{8,0},{12,4},{16,24},{20,28},{24,16},{28,20},{1,9},{5... | collective-permute-start | bytes 393224 | tf_op jit(solution)/shard_map/ppermute | solution.py:21
  20.2 12.7 %collective-permute-start.2 = (bf16[4,64,512]{2,1,0:T(8,128)(2,1)S(1)}, bf16[4,64,512]{2,1,0:T(8,128)(2,1)S(1)}, u32[]{:S(2)}, u32[]{:S(2)}) collective-permute-start(bf16[4,64,512]{2,1,0:T(8,128)(2,1)S(1)} %pad_maximum_fusion), channel_id=1, source_target_pairs={{0,16},{4,20},{8,24},{12,28},{16,0},{20,4},{24,8},{28,12},{1,17},{... | collective-permute-start | bytes 786440 | tf_op jit(solution)/shard_map/ppermute | solution.py:21
  56.4 24.8 %copy-start.1 = (bf16[64,512]{1,0:T(8,128)(2,1)S(1)}, bf16[64,512]{1,0:T(8,128)(2,1)}, u32[]{:S(2)}) copy-start(bf16[64,512]{1,0:T(8,128)(2,1)} %param.5) | copy-start | bytes 196612
Sparse Core Ops, SparseCore 0:
  58.3 22.8 reduce-scatter.1
